TPU v7x, 32 devices: a whole 2x2x4 slice. The times are simulated.
32 devices in a mesh: dp: 2 (over y), ctx: 4 (over x, core), tp: 4 (over z).
Axes of the slice: x: 2, y: 2, z: 4, core: 2. Of those that a mesh axis runs over, the one named last changes fastest.
Arguments:
- layer_input: bfloat16 [2, 2048, 1024], P('dp', 'ctx'), may hold values from -6 to 6
- cotangent: bfloat16 [2, 2048, 1024], P('dp', 'ctx'), may hold values from -6 to 6
- segment_ids: int32 [2, 2048], P('dp'), may hold values from 0 to 11, never falling along the last dimension, each value on 1 to 1536 neighbouring positions
- norm1_gain: bfloat16 [1024], P(('dp', 'ctx')), may hold values from 0.5 to 1.5
- norm1_bias: bfloat16 [1024], P(('dp', 'ctx')), may hold values from -3 to 3
- attend_weight: bfloat16 [1024, 3, 1024], P(('dp', 'ctx'), None, 'tp'), may hold values from -0.1875 to 0.1875
- attend_bias: bfloat16 [2, 1024], P(None, ('tp', 'dp', 'ctx')), may hold values from -3 to 3
- merge_weight: bfloat16 [1024, 1024], P('tp', ('dp', 'ctx')), may hold values from -0.75 to 0.75
- merge_bias: bfloat16 [1024], P(('dp', 'ctx')), may hold values from -3 to 3
- norm2_gain: bfloat16 [1024], P(('dp', 'ctx')), may hold values from 0.5 to 1.5
- norm2_bias: bfloat16 [1024], P(('dp', 'ctx')), may hold values from -3 to 3
- expand_weight: bfloat16 [1024, 4096], P(('dp', 'ctx'), 'tp'), may hold values from -0.1875 to 0.1875
- expand_bias: bfloat16 [4096], P(('tp', 'dp', 'ctx')), may hold values from -3 to 3
- shrink_weight: bfloat16 [4096, 1024], P('tp', ('dp', 'ctx')), may hold values from -0.09375 to 0.09375
- shrink_bias: bfloat16 [1024], P(('dp', 'ctx')), may hold values from -3 to 3
Outputs:
- layer_output: bfloat16 [2, 2048, 1024], P('dp', 'ctx')
- input_grad: bfloat16 [2, 2048, 1024], P('dp', 'ctx')
- grad_norm1_gain: float32 [1024], P(('dp', 'ctx'))
- grad_norm1_bias: float32 [1024], P(('dp', 'ctx'))
- grad_attend_weight: float32 [1024, 3, 1024], P(('dp', 'ctx'), None, 'tp')
- grad_attend_bias: float32 [2, 1024], P(None, ('tp', 'dp', 'ctx'))
- grad_merge_weight: float32 [1024, 1024], P('tp', ('dp', 'ctx'))
- grad_merge_bias: float32 [1024], P(('dp', 'ctx'))
- grad_norm2_gain: float32 [1024], P(('dp', 'ctx'))
- grad_norm2_bias: float32 [1024], P(('dp', 'ctx'))
- grad_expand_weight: float32 [1024, 4096], P(('dp', 'ctx'), 'tp')
- grad_expand_bias: float32 [4096], P(('tp', 'dp', 'ctx'))
- grad_shrink_weight: float32 [4096, 1024], P('tp', ('dp', 'ctx'))
- grad_shrink_bias: float32 [1024], P(('dp', 'ctx'))
Inputs may be any that keep to these rules, and one draw needn't show every extreme that they name: `segment_ids`: within each sequence the segment number never falls; every number 0 to 11 occurs; each holds 1 to 1536 tokens and one holds exactly 1536; segment 0, at the start of a sequence, is padding.
All inputs are finite; a program needn't handle non-finite values.
Results may differ from a plain program's by a relative error of at most 0.02.
Values may be sent and summed in bfloat16 or wider, within the bound.
No kernel may reach another device: no remote copies, remote signals or barrier semaphores. Data moves between devices by JAX's collectives and lax.ppermute only.
A program may use at most 128 MiB of HBM per device.

v0:
```python
import math
import jax
import jax.numpy as jnp
from jax import lax
from jax.sharding import PartitionSpec as P

HD = 64


def norm_forward(values, gain, bias):
    row_mean = jnp.mean(values, axis=-1, keepdims=True)
    centered = values - row_mean
    row_var = jnp.mean(centered * centered, axis=-1, keepdims=True)
    inv_std = lax.rsqrt(row_var + 1e-05)
    normal = centered * inv_std
    return (normal * gain + bias, normal, inv_std)


def norm_backward(grad_out, normal, inv_std, gain):
    grad_normal = grad_out * gain
    centered_grad = grad_normal - jnp.mean(grad_normal, axis=-1, keepdims=True)
    return inv_std * (
        centered_grad - normal * jnp.mean(grad_normal * normal, axis=-1, keepdims=True)
    )


def gelu_tanh(values):
    return (
        0.5
        * values
        * (1.0 + jnp.tanh(0.7978845608028654 * (values + 0.044715 * values * values * values)))
    )


def token_sum(values):
    return jnp.sum(values, axis=(0, 1))


def body(
    layer_input,
    cotangent,
    segment_ids,
    norm1_gain,
    norm1_bias,
    attend_weight,
    attend_bias,
    merge_weight,
    merge_bias,
    norm2_gain,
    norm2_bias,
    expand_weight,
    expand_bias,
    shrink_weight,
    shrink_bias,
):
    fwd_params = (
        lax.all_gather(norm1_gain, ("dp", "ctx"), axis=0, tiled=True),
        lax.all_gather(norm1_bias, ("dp", "ctx"), axis=0, tiled=True),
        lax.all_gather(attend_weight, ("dp", "ctx"), axis=0, tiled=True),
        lax.all_gather(attend_bias, ("dp", "ctx"), axis=1, tiled=True),
        lax.all_gather(merge_weight, ("dp", "ctx"), axis=1, tiled=True),
        lax.all_gather(merge_bias, ("dp", "ctx"), axis=0, tiled=True),
        lax.all_gather(norm2_gain, ("dp", "ctx"), axis=0, tiled=True),
        lax.all_gather(norm2_bias, ("dp", "ctx"), axis=0, tiled=True),
        lax.all_gather(expand_weight, ("dp", "ctx"), axis=0, tiled=True),
        lax.all_gather(expand_bias, ("dp", "ctx"), axis=0, tiled=True),
        lax.all_gather(shrink_weight, ("dp", "ctx"), axis=1, tiled=True),
        lax.all_gather(shrink_bias, ("dp", "ctx"), axis=0, tiled=True),
    )
    gain_one = fwd_params[0].astype(jnp.float32)
    bias_one = fwd_params[1].astype(jnp.float32)
    attention_full_weight = fwd_params[2]
    attend_add = fwd_params[3].astype(jnp.float32)
    merge_full = fwd_params[4]
    merge_add = fwd_params[5].astype(jnp.float32)
    gain_two = fwd_params[6].astype(jnp.float32)
    bias_two = fwd_params[7].astype(jnp.float32)
    expand_full = fwd_params[8]
    expand_add = fwd_params[9].astype(jnp.float32)
    shrink_full = fwd_params[10]
    shrink_add = fwd_params[11].astype(jnp.float32)
    seq_count, q_len, model_width = layer_input.shape
    length = segment_ids.shape[1]
    local_width = attention_full_weight.shape[2]
    heads_local = local_width // HD
    head_scale_factor = 1.0 / math.sqrt(HD)
    ctx_start = lax.axis_index("ctx") * q_len
    inputs = layer_input.astype(jnp.float32)
    norm_out, normal_one, inv_one = norm_forward(inputs, gain_one, bias_one)
    normalized_input = norm_out.astype(jnp.bfloat16)
    projected_rows = jnp.einsum(
        "bhv,vrw->bhrw", normalized_input, attention_full_weight, preferred_element_type=jnp.float32
    )
    query = (projected_rows[:, :, 0] + attend_add[0]).astype(jnp.bfloat16)
    key_local = projected_rows[:, :, 1].astype(jnp.bfloat16)
    value_local = (projected_rows[:, :, 2] + attend_add[1]).astype(jnp.bfloat16)
    keys_all, values_all = (
        lax.all_gather(key_local, "ctx", axis=1, tiled=True),
        lax.all_gather(value_local, "ctx", axis=1, tiled=True),
    )
    seg_query = lax.dynamic_slice_in_dim(segment_ids, ctx_start, q_len, 1)
    query_pos = ctx_start + lax.iota(jnp.int32, q_len)
    key_pos = lax.iota(jnp.int32, length)
    allowed = (seg_query[:, :, None] == segment_ids[:, None, :]) & (
        key_pos[None, None, :] <= query_pos[None, :, None]
    )
    head_outs = []
    lse_list = []
    for head in range(heads_local):
        columns = slice(head * HD, (head + 1) * HD)
        unnormalized_scores = (
            jnp.einsum(
                "sqd,skd->sqk",
                query[..., columns],
                keys_all[..., columns],
                preferred_element_type=jnp.float32,
            )
            * head_scale_factor
        )
        scores = jnp.where(allowed, unnormalized_scores, -1e30)
        row_top = jnp.max(scores, axis=-1, keepdims=True)
        exp_scores = jnp.exp(scores - row_top)
        row_total = jnp.sum(exp_scores, axis=-1, keepdims=True)
        softmax_probabilities = (exp_scores / row_total).astype(jnp.bfloat16)
        head_outs.append(
            jnp.einsum(
                "sqk,skd->sqd",
                softmax_probabilities,
                values_all[..., columns],
                preferred_element_type=jnp.float32,
            )
        )
        lse_list.append(row_top + jnp.log(row_total))
    mixed = jnp.concatenate(head_outs, axis=-1).astype(jnp.bfloat16)
    attn_part = jnp.einsum("sqm,md->sqd", mixed, merge_full, preferred_element_type=jnp.float32)
    attn_out = lax.psum(attn_part.astype(jnp.bfloat16), "tp").astype(jnp.float32)
    hidden = inputs + attn_out + merge_add
    norm_two, normal_two, inv_two = norm_forward(hidden, gain_two, bias_two)
    normed2 = norm_two.astype(jnp.bfloat16)
    pre_act = (
        jnp.einsum("sqd,df->sqf", normed2, expand_full, preferred_element_type=jnp.float32)
        + expand_add
    )
    act_value, gelu_pull = jax.vjp(gelu_tanh, pre_act)
    activation = act_value.astype(jnp.bfloat16)
    mlp_part = jnp.einsum(
        "sqf,fd->sqd", activation, shrink_full, preferred_element_type=jnp.float32
    )
    mlp_out = lax.psum(mlp_part.astype(jnp.bfloat16), "tp").astype(jnp.float32)
    layer_output = (hidden + mlp_out + shrink_add).astype(jnp.bfloat16)
    back_params = (
        lax.all_gather(norm1_gain, ("dp", "ctx"), axis=0, tiled=True),
        lax.all_gather(norm1_bias, ("dp", "ctx"), axis=0, tiled=True),
        lax.all_gather(attend_weight, ("dp", "ctx"), axis=0, tiled=True),
        lax.all_gather(attend_bias, ("dp", "ctx"), axis=1, tiled=True),
        lax.all_gather(merge_weight, ("dp", "ctx"), axis=1, tiled=True),
        lax.all_gather(merge_bias, ("dp", "ctx"), axis=0, tiled=True),
        lax.all_gather(norm2_gain, ("dp", "ctx"), axis=0, tiled=True),
        lax.all_gather(norm2_bias, ("dp", "ctx"), axis=0, tiled=True),
        lax.all_gather(expand_weight, ("dp", "ctx"), axis=0, tiled=True),
        lax.all_gather(expand_bias, ("dp", "ctx"), axis=0, tiled=True),
        lax.all_gather(shrink_weight, ("dp", "ctx"), axis=1, tiled=True),
        lax.all_gather(shrink_bias, ("dp", "ctx"), axis=0, tiled=True),
    )
    gain_one = back_params[0].astype(jnp.float32)
    attention_full_weight = back_params[2]
    merge_full = back_params[4]
    gain_two = back_params[6].astype(jnp.float32)
    expand_full = back_params[8]
    shrink_full = back_params[10]
    keys_all, values_all = (
        lax.all_gather(key_local, "ctx", axis=1, tiled=True),
        lax.all_gather(value_local, "ctx", axis=1, tiled=True),
    )
    keep_mask = (seg_query > 0).astype(jnp.float32)
    grad_y = cotangent.astype(jnp.float32) * keep_mask[:, :, None]
    grad_y_low = grad_y.astype(jnp.bfloat16)
    grad_shrink_w = jnp.einsum(
        "sqf,sqd->fd", activation, grad_y_low, preferred_element_type=jnp.float32
    )
    grad_shrink_b = token_sum(grad_y)
    grad_act = jnp.einsum(
        "sqd,fd->sqf", grad_y_low, shrink_full, preferred_element_type=jnp.float32
    )
    grad_pre = gelu_pull(grad_act)[0].astype(jnp.bfloat16)
    grad_expand_w = jnp.einsum("sqd,sqf->df", normed2, grad_pre, preferred_element_type=jnp.float32)
    grad_expand_b = token_sum(grad_pre.astype(jnp.float32))
    normed2_part = jnp.einsum(
        "sqf,df->sqd", grad_pre, expand_full, preferred_element_type=jnp.float32
    )
    grad_normed2 = lax.psum(normed2_part.astype(jnp.bfloat16), "tp").astype(jnp.float32)
    grad_hidden = grad_y + norm_backward(grad_normed2, normal_two, inv_two, gain_two)
    grad_attn = grad_hidden.astype(jnp.bfloat16)
    grad_norm2_g = token_sum(grad_normed2 * normal_two)
    grad_norm2_b = token_sum(grad_normed2)
    grad_merge_b = token_sum(grad_hidden)
    grad_merge_w = jnp.einsum("sqm,sqd->md", mixed, grad_attn, preferred_element_type=jnp.float32)
    grad_mixed = jnp.einsum(
        "sqd,md->sqm", grad_attn, merge_full, preferred_element_type=jnp.float32
    ).astype(jnp.bfloat16)
    query_grads = []
    key_grads = []
    value_grads = []
    for head in range(heads_local):
        columns = slice(head * HD, (head + 1) * HD)
        query_per_head = query[..., columns]
        key_per_head = keys_all[..., columns]
        value_per_head = values_all[..., columns]
        grad_out_h = grad_mixed[..., columns]
        unnormalized_scores = (
            jnp.einsum(
                "sqd,skd->sqk", query_per_head, key_per_head, preferred_element_type=jnp.float32
            )
            * head_scale_factor
        )
        softmax_f = jnp.where(allowed, jnp.exp(unnormalized_scores - lse_list[head]), 0.0)
        softmax_probabilities = softmax_f.astype(jnp.bfloat16)
        value_grads.append(
            jnp.einsum(
                "sqk,sqd->skd",
                softmax_probabilities,
                grad_out_h,
                preferred_element_type=jnp.float32,
            )
        )
        grad_probs = jnp.einsum(
            "sqd,skd->sqk", grad_out_h, value_per_head, preferred_element_type=jnp.float32
        )
        inner = jnp.sum(softmax_f * grad_probs, axis=-1, keepdims=True)
        grad_scores = (softmax_f * (grad_probs - inner)).astype(jnp.bfloat16)
        query_grads.append(
            jnp.einsum(
                "sqk,skd->sqd", grad_scores, key_per_head, preferred_element_type=jnp.float32
            )
            * head_scale_factor
        )
        key_grads.append(
            jnp.einsum(
                "sqk,sqd->skd", grad_scores, query_per_head, preferred_element_type=jnp.float32
            )
            * head_scale_factor
        )
    grad_query = jnp.concatenate(query_grads, axis=-1).astype(jnp.bfloat16)
    grad_key_sum, grad_value_sum = (
        lax.psum_scatter(
            jnp.concatenate(key_grads, axis=-1).astype(jnp.bfloat16),
            "ctx",
            scatter_dimension=1,
            tiled=True,
        ).astype(jnp.float32),
        lax.psum_scatter(
            jnp.concatenate(value_grads, axis=-1).astype(jnp.bfloat16),
            "ctx",
            scatter_dimension=1,
            tiled=True,
        ).astype(jnp.float32),
    )
    grad_proj = jnp.stack(
        (grad_query, grad_key_sum.astype(jnp.bfloat16), grad_value_sum.astype(jnp.bfloat16)), axis=2
    )
    grad_attend_w = jnp.einsum(
        "sqd,sqcm->dcm", normalized_input, grad_proj, preferred_element_type=jnp.float32
    )
    grad_proj_f = grad_proj.astype(jnp.float32)
    grad_attend_b = jnp.stack(
        (token_sum(grad_proj_f[:, :, 0]), token_sum(grad_proj_f[:, :, 2])), axis=0
    )
    normed1_part = jnp.einsum(
        "sqcm,dcm->sqd", grad_proj, attention_full_weight, preferred_element_type=jnp.float32
    )
    grad_normed1 = lax.psum(normed1_part.astype(jnp.bfloat16), "tp").astype(jnp.float32)
    grad_norm1_g = token_sum(grad_normed1 * normal_one)
    grad_norm1_b = token_sum(grad_normed1)
    input_grad = (grad_hidden + norm_backward(grad_normed1, normal_one, inv_one, gain_one)).astype(
        jnp.bfloat16
    )
    shards = (
        lax.psum_scatter(grad_norm1_g, ("dp", "ctx"), scatter_dimension=0, tiled=True),
        lax.psum_scatter(grad_norm1_b, ("dp", "ctx"), scatter_dimension=0, tiled=True),
        lax.psum_scatter(grad_attend_w, ("dp", "ctx"), scatter_dimension=0, tiled=True),
        lax.psum_scatter(grad_attend_b, ("dp", "ctx"), scatter_dimension=1, tiled=True),
        lax.psum_scatter(grad_merge_w, ("dp", "ctx"), scatter_dimension=1, tiled=True),
        lax.psum_scatter(grad_merge_b, ("dp", "ctx"), scatter_dimension=0, tiled=True),
        lax.psum_scatter(grad_norm2_g, ("dp", "ctx"), scatter_dimension=0, tiled=True),
        lax.psum_scatter(grad_norm2_b, ("dp", "ctx"), scatter_dimension=0, tiled=True),
        lax.psum_scatter(grad_expand_w, ("dp", "ctx"), scatter_dimension=0, tiled=True),
        lax.psum_scatter(grad_expand_b, ("dp", "ctx"), scatter_dimension=0, tiled=True),
        lax.psum_scatter(grad_shrink_w, ("dp", "ctx"), scatter_dimension=1, tiled=True),
        lax.psum_scatter(grad_shrink_b, ("dp", "ctx"), scatter_dimension=0, tiled=True),
    )
    return (
        layer_output,
        input_grad,
        shards[0],
        shards[1],
        shards[2],
        shards[3],
        shards[4],
        shards[5],
        shards[6],
        shards[7],
        shards[8],
        shards[9],
        shards[10],
        shards[11],
    )


def solution(mesh):
    return jax.shard_map(
        body,
        mesh=mesh,
        in_specs=(
            P("dp", "ctx", None),
            P("dp", "ctx", None),
            P("dp", None),
            P(("dp", "ctx")),
            P(("dp", "ctx")),
            P(("dp", "ctx"), None, "tp"),
            P(None, ("tp", "dp", "ctx")),
            P("tp", ("dp", "ctx")),
            P(("dp", "ctx")),
            P(("dp", "ctx")),
            P(("dp", "ctx")),
            P(("dp", "ctx"), "tp"),
            P(("tp", "dp", "ctx")),
            P("tp", ("dp", "ctx")),
            P(("dp", "ctx")),
        ),
        out_specs=(
            P("dp", "ctx", None),
            P("dp", "ctx", None),
            P(("dp", "ctx")),
            P(("dp", "ctx")),
            P(("dp", "ctx"), None, "tp"),
            P(None, ("tp", "dp", "ctx")),
            P("tp", ("dp", "ctx")),
            P(("dp", "ctx")),
            P(("dp", "ctx")),
            P(("dp", "ctx")),
            P(("dp", "ctx"), "tp"),
            P(("tp", "dp", "ctx")),
            P("tp", ("dp", "ctx")),
            P(("dp", "ctx")),
        ),
        check_vma=False,
    )
```

profile of v0, /device:TPU:0, one launch (start us, length us, event | category | flops | bytes accessed | tf_op | source)
XLA Modules:
  0.0 676.2 jit_solution(15304905114799007541)
XLA Ops:
  9.1 10.3 %all-gather.1 = bf16[8,1,128]{2,1,0:T(2,128)(2,1)S(1)} all-gather(bf16[1,1,128]{2,1,0:T(2,128)(2,1)} %bitcast.294), channel_id=1, replica_groups=mesh['dp'=2,'ctx'=4,'tp'=4] {'dp','ctx'}, dimensions={0}, use_global_device_ids=true | all-gather | bytes 2304 | tf_op jit(solution)/shard_map/all_gather | solution.py:57
  19.4 8.6 %all-gather.2 = bf16[8,1,128]{2,1,0:T(2,128)(2,1)S(1)} all-gather(bf16[1,1,128]{2,1,0:T(2,128)(2,1)} %bitcast.295), channel_id=1, replica_groups=mesh['dp'=2,'ctx'=4,'tp'=4] {'dp','ctx'}, dimensions={0}, use_global_device_ids=true | all-gather | bytes 2304 | tf_op jit(solution)/shard_map/all_gather | solution.py:58
  30.0 9.1 %all-gather.15.cloned.1.call-done = bf16[1024,3,256]{0,2,1:T(8,128)(2,1)} async-done(((bf16[128,3,256]{0,2,1:T(8,128)(2,1)}), bf16[1024,3,256]{0,2,1:T(8,128)(2,1)}) %all-gather.15.cloned.1.call-update) | async-done | bytes 1572880 | tf_op jit(solution)/shard_map/all_gather | solution.py:59
  43.8 8.7 %all-gather.3 = bf16[8,32,2]{1,2,0:T(2,128)(2,1)S(1)} all-gather(bf16[1,32,2]{1,2,0:T(2,128)(2,1)S(1)} %bitcast.296), channel_id=1, replica_groups=mesh['dp'=2,'ctx'=4,'tp'=4] {'dp','ctx'}, dimensions={0}, use_global_device_ids=true | all-gather | bytes 1152 | tf_op jit(solution)/shard_map/all_gather | solution.py:60
  52.6 9.8 %all_gather.56 = bf16[256,1024]{1,0:T(8,128)(2,1)S(1)} all-gather(bf16[256,128]{1,0:T(8,128)(2,1)S(1)} %copy-done.43), channel_id=1, replica_groups=mesh['dp'=2,'ctx'=4,'tp'=4] {'dp','ctx'}, dimensions={1}, use_global_device_ids=true | all-gather | bytes 589824 | tf_op jit(solution)/shard_map/all_gather | solution.py:61
  73.6 4.4 fusion.2
  81.4 4.0 fusion.72
  94.4 8.7 %all-gather.4 = bf16[8,1,128]{2,1,0:T(2,128)(2,1)S(1)} all-gather(bf16[1,1,128]{2,1,0:T(2,128)(2,1)S(1)} %bitcast.297), channel_id=1, replica_groups=mesh['dp'=2,'ctx'=4,'tp'=4] {'dp','ctx'}, dimensions={0}, use_global_device_ids=true | all-gather | bytes 2304 | tf_op jit(solution)/shard_map/all_gather | solution.py:62
  103.1 7.8 %all-gather.5 = bf16[8,1,128]{2,1,0:T(2,128)(2,1)S(1)} all-gather(bf16[1,1,128]{2,1,0:T(2,128)(2,1)S(1)} %bitcast.298), channel_id=1, replica_groups=mesh['dp'=2,'ctx'=4,'tp'=4] {'dp','ctx'}, dimensions={0}, use_global_device_ids=true | all-gather | bytes 2304 | tf_op jit(solution)/shard_map/all_gather | solution.py:63
  110.9 8.7 %all-gather.6 = bf16[8,1,128]{2,1,0:T(2,128)(2,1)S(1)} all-gather(bf16[1,1,128]{2,1,0:T(2,128)(2,1)S(1)} %bitcast.299), channel_id=1, replica_groups=mesh['dp'=2,'ctx'=4,'tp'=4] {'dp','ctx'}, dimensions={0}, use_global_device_ids=true | all-gather | bytes 2304 | tf_op jit(solution)/shard_map/all_gather | solution.py:64
  119.6 8.0 %all-gather.7 = bf16[8,1,128]{2,1,0:T(2,128)(2,1)S(1)} all-gather(bf16[1,1,128]{2,1,0:T(2,128)(2,1)S(1)} %bitcast.300), channel_id=1, replica_groups=mesh['dp'=2,'ctx'=4,'tp'=4] {'dp','ctx'}, dimensions={0}, use_global_device_ids=true | all-gather | bytes 2304 | tf_op jit(solution)/shard_map/all_gather | solution.py:66
  127.6 17.5 %all-reduce.13.cloned.1.call-done = bf16[1,512,1024]{2,1,0:T(8,128)(2,1)} async-done(((bf16[1,512,1024]{2,1,0:T(8,128)(2,1)}), bf16[1,512,1024]{2,1,0:T(8,128)(2,1)}) %all-reduce.13.cloned.1.call-update) | async-done | bytes 1048592 | tf_op jit(solution)/shard_map/psum | solution.py:136
  147.5 26.9 %all-gather.19.cloned.1.call-done = bf16[1024,1024]{1,0:T(8,128)(2,1)} async-done(((bf16[128,1024]{1,0:T(8,128)(2,1)}), bf16[1024,1024]{1,0:T(8,128)(2,1)}) %all-gather.19.cloned.1.call-update) | async-done | bytes 2097168 | tf_op jit(solution)/shard_map/all_gather | solution.py:65
  174.3 4.3 fusion.121
  178.6 25.9 %all-gather.21.cloned.1.call-done = bf16[1024,1024]{1,0:T(8,128)(2,1)} async-done(((bf16[1024,128]{1,0:T(8,128)(2,1)}), bf16[1024,1024]{1,0:T(8,128)(2,1)}) %all-gather.21.cloned.1.call-update) | async-done | bytes 2097168 | tf_op jit(solution)/shard_map/all_gather | solution.py:67
  204.4 6.1 convert_reduce_fusion.3
  214.2 51.6 %all-reduce.15.cloned.1.call-done = bf16[1,512,1024]{2,1,0:T(8,128)(2,1)} async-done(((bf16[1,512,1024]{2,1,0:T(8,128)(2,1)}), bf16[1,512,1024]{2,1,0:T(8,128)(2,1)}) %all-reduce.15.cloned.1.call-update) | async-done | bytes 1048592 | tf_op jit(solution)/shard_map/psum | solution.py:191
  291.3 9.1 %multiply_reduce_fusion.3 = (f32[512]{0:T(512)S(1)}, f32[512]{0:T(512)S(1)}, f32[512]{0:T(512)S(1)}, f32[512]{0:T(512)S(1)}, f32[512,2048]{1,0:T(8,128)}) fusion(f32[512]{0:T(512)S(1)} %get-tuple-element.68, f32[512,2048]{1,0:T(8,128)} %copy-done.22, s32[512]{0:T(512)S(1)} %iota_add_fusion, s32[2048]{0:T(1024)S(1)} %bitcast.254, s32[512]{0:T(512)S(1)} %bitcast.275, ...), kind=kOutput, calls=%fused_computation.10 | convolution fusion | flops 158332928 | bytes 33910784 | tf_op jit(solution)/shard_map/sqd,skd->sqk/dot_general | solution.py:226
  300.4 13.1 %multiply_convert_fusion.3 = (bf16[512,2048]{1,0:T(8,128)(2,1)}, bf16[512,2048]{1,0:T(8,128)(2,1)}, bf16[512,2048]{1,0:T(8,128)(2,1)}, bf16[512,2048]{1,0:T(8,128)(2,1)}) fusion(f32[512,2048]{1,0:T(8,128)} %get-tuple-element.62, f32[512]{0:T(512)S(1)} %get-tuple-element.24, f32[512]{0:T(512)S(1)} %get-tuple-element.68, f32[512,2048]{1,0:T(8,128)} %copy-done.22, ...), kind=kLoop, calls=%fused_computation.9 | loop fusion | flops 28311552 | bytes 41971712 | tf_op jit(solution)/shard_map/convert_element_type | solution.py:230
  319.1 4.8 fusion.64
  327.8 15.7 %reduce-scatter.10.cloned.1.call-done = bf16[1,512,256]{1,2,0:T(8,128)(2,1)} async-done(((bf16[1,2048,256]{1,2,0:T(8,128)(2,1)}), bf16[1,512,256]{1,2,0:T(8,128)(2,1)}) %reduce-scatter.10.cloned.1.call-update) | async-done | bytes 262160 | tf_op jit(solution)/shard_map/reduce_scatter | solution.py:245
  353.4 5.6 fusion.90
  359.0 4.9 fusion.119
  364.7 3.9 fusion.114
  369.3 8.7 %all-gather.8 = bf16[8,1,128]{2,1,0:T(2,128)(2,1)S(1)} all-gather(bf16[1,1,128]{2,1,0:T(2,128)(2,1)S(1)} %bitcast.301), channel_id=1, replica_groups=mesh['dp'=2,'ctx'=4,'tp'=4] {'dp','ctx'}, dimensions={0}, use_global_device_ids=true | all-gather | bytes 2304 | tf_op jit(solution)/shard_map/all_gather | solution.py:68
  381.1 88.9 %all-reduce.17.cloned.1.call-done = (bf16[1,512,1024]{2,1,0:T(8,128)(2,1)}, bf16[1,512,1024]{2,1,0:T(8,128)(2,1)}) async-done(((bf16[1,512,1024]{2,1,0:T(8,128)(2,1)}, bf16[1,512,1024]{2,1,0:T(8,128)(2,1)}), (bf16[1,512,1024]{2,1,0:T(8,128)(2,1)}, bf16[1,512,1024]{2,1,0:T(8,128)(2,1)})) %all-reduce.17.cloned.1.call-update) | async-done | bytes 2097168 | tf_op jit(solution)/shard_map/psum | solution.py:149
  472.3 24.2 %all-reduce.7 = (f32[1024]{0:T(1024)S(1)}, f32[1024]{0:T(1024)S(1)}, f32[1024]{0:T(1024)S(1)}, f32[1024]{0:T(1024)S(1)}, f32[1024]{0:T(1024)S(1)}, /*index=5*/f32[1024]{0:T(1024)S(1)}, f32[1024]{0:T(1024)S(1)}) all-reduce(f32[1024]{0:T(1024)S(1)} %get-tuple-element.16, ...), channel_id=5, replica_groups=mesh['dp'=2,'ctx'=4,'tp'=4] {'dp','ctx'}, use_global_device_ids=true, to_apply=%region_27.28.clone | all-reduce | flops 7168 | bytes 57344
  500.5 3.6 fusion.36
  504.1 4.5 reduce-scatter.16.cloned.1.call-done
  508.6 55.3 %reduce-scatter.20.cloned.1.call-done = f32[1024,128]{1,0:T(8,128)} async-done(((f32[1024,1024]{1,0:T(8,128)}), f32[1024,128]{1,0:T(8,128)}) %reduce-scatter.20.cloned.1.call-update) | async-done | bytes 524304 | tf_op jit(solution)/shard_map/reduce_scatter | solution.py:288
  563.9 55.5 %reduce-scatter.18.cloned.1.call-done = f32[128,1024]{1,0:T(8,128)} async-done(((f32[1024,1024]{1,0:T(8,128)}), f32[128,1024]{1,0:T(8,128)}) %reduce-scatter.18.cloned.1.call-update) | async-done | bytes 524304 | tf_op jit(solution)/shard_map/reduce_scatter | solution.py:286
  619.4 50.1 %reduce-scatter.14.cloned.1.call-done = f32[128,3,256]{2,0,1:T(8,128)} async-done(((f32[1024,3,256]{2,0,1:T(8,128)}), f32[128,3,256]{2,0,1:T(8,128)}) %reduce-scatter.14.cloned.1.call-update) | async-done | bytes 393232 | tf_op jit(solution)/shard_map/reduce_scatter | solution.py:280
  (243 shorter events, 92.3 us)
Async XLA Ops:
  7.2 22.3 %copy-start.7 = (bf16[1,512,1024]{2,1,0:T(8,128)(2,1)S(1)}, bf16[1,512,1024]{2,1,0:T(8,128)(2,1)}, u32[]{:S(2)}) copy-start(bf16[1,512,1024]{2,1,0:T(8,128)(2,1)} %param.15) | copy-start | bytes 3145732
  7.2 31.9 %all-gather.15.cloned.1.call-start = ((), (), s32[]{:S(2)}) async-start(), calls=%async_computation.7 | async-start | bytes 1769472 | tf_op jit(solution)/shard_map/all_gather | solution.py:59
  9.1 55.5 %all-gather.23.cloned.1.call-start = ((), (), s32[]{:S(2)}) async-start(), calls=%async_computation.19 | async-start | bytes 1310720 | tf_op jit(solution)/shard_map/all_gather | solution.py:98
  28.1 13.7 %copy-start.55 = (f32[8,1,128]{2,1,0:T(1,128)}, f32[8,1,128]{2,1,0:T(1,128)S(1)}, u32[]{:S(2)}) copy-start(f32[8,1,128]{2,1,0:T(1,128)S(1)} %convert_element_type.298) | copy-start | bytes 12292
  43.7 37.7 %all-gather.17.cloned.1.call-start = ((), (), s32[]{:S(2)}) async-start(), calls=%async_computation.8 | async-start | bytes 1310720 | tf_op jit(solution)/shard_map/all_gather | solution.py:99
  52.6 216.4 %copy-start.53 = (f32[1,512]{1,0:T(1,128)}, f32[1,512]{1,0:T(1,128)S(1)}, u32[]{:S(2)}) copy-start(f32[1,512]{1,0:T(1,128)S(1)} %get-tuple-element.46) | copy-start | bytes 6148
  64.5 80.6 %all-reduce.13.cloned.1.call-start = ((), (), s32[]{:S(2)}) async-start(), calls=%async_computation.9 | async-start | bytes 2097152 | tf_op jit(solution)/shard_map/psum | solution.py:136
  91.6 55.2 %copy-start.41 = (bf16[512,64]{0,1:T(8,128)(2,1)}, bf16[512,64]{0,1:T(8,128)(2,1)S(1)}, u32[]{:S(2)}) copy-start(bf16[512,64]{0,1:T(8,128)(2,1)S(1)} %fusion.73) | copy-start | bytes 196612
  91.6 19.2 %copy-start.61 = (bf16[128]{0:T(256)(128)(2,1)S(1)}, bf16[128]{0:T(256)(128)(2,1)}, u32[]{:S(2)}) copy-start(bf16[128]{0:T(256)(128)(2,1)} %param.25) | copy-start | bytes 772
  91.7 27.9 %copy-start.62 = (bf16[128]{0:T(256)(128)(2,1)S(1)}, bf16[128]{0:T(256)(128)(2,1)}, u32[]{:S(2)}) copy-start(bf16[128]{0:T(256)(128)(2,1)} %param.27) | copy-start | bytes 772
  93.1 81.2 %all-gather.19.cloned.1.call-start = ((), (), s32[]{:S(2)}) async-start(), calls=%async_computation.10 | async-start | bytes 2359296 | tf_op jit(solution)/shard_map/all_gather | solution.py:65
  93.7 110.7 %all-gather.21.cloned.1.call-start = ((), (), s32[]{:S(2)}) async-start(), calls=%async_computation.11 | async-start | bytes 2359296 | tf_op jit(solution)/shard_map/all_gather | solution.py:67
  94.3 171.5 %all-reduce.15.cloned.1.call-start = ((), (), s32[]{:S(2)}) async-start(), calls=%async_computation.12 | async-start | bytes 2097152 | tf_op jit(solution)/shard_map/psum | solution.py:191
  119.6 54.8 %copy-start.56 = (f32[8,1,128]{2,1,0:T(1,128)}, f32[8,1,128]{2,1,0:T(1,128)S(1)}, u32[]{:S(2)}) copy-start(f32[8,1,128]{2,1,0:T(1,128)S(1)} %convert_element_type.302) | copy-start | bytes 12292
  127.6 191.5 %copy-start.57 = (f32[8,1,128]{2,1,0:T(1,128)}, f32[8,1,128]{2,1,0:T(1,128)S(1)}, u32[]{:S(2)}) copy-start(f32[8,1,128]{2,1,0:T(1,128)S(1)} %convert_element_type.303) | copy-start | bytes 12292
  147.4 121.6 %copy-start.46 = (f32[512]{0:T(512)}, f32[512]{0:T(512)S(1)}, u32[]{:S(2)}) copy-start(f32[512]{0:T(512)S(1)} %add_rsqrt_fusion) | copy-start | bytes 6148
  213.9 113.9 %reduce-scatter.12.cloned.1.call-start = ((), (), s32[]{:S(2)}) async-start(), calls=%async_computation.14 | async-start | bytes 1310720 | tf_op jit(solution)/shard_map/reduce_scatter | solution.py:251
  281.5 62.0 %reduce-scatter.10.cloned.1.call-start = ((), (), s32[]{:S(2)}) async-start(), calls=%async_computation.13 | async-start | bytes 1310720 | tf_op jit(solution)/shard_map/reduce_scatter | solution.py:245
  319.0 60.7 %reduce-scatter.22.cloned.1.call-start = ((), (), s32[]{:S(2)}) async-start(), calls=%async_computation.20 | async-start | bytes 147456
  327.8 18.1 %copy-start.32 = (bf16[1,512,256]{1,2,0:T(8,128)(2,1)S(1)}, bf16[1,512,256]{1,2,0:T(8,128)(2,1)}, u32[]{:S(2)}) copy-start(bf16[1,512,256]{1,2,0:T(8,128)(2,1)} %reduce-scatter.12.cloned.1.call-done) | copy-start | bytes 786436
  327.8 18.1 %copy-start.35 = (bf16[512,64]{0,1:T(8,128)(2,1)S(1)}, bf16[512,64]{0,1:T(8,128)(2,1)}, u32[]{:S(2)}) copy-start(bf16[512,64]{0,1:T(8,128)(2,1)} %copy-done.34) | copy-start | bytes 196612
  327.8 18.1 %copy-start.37 = (bf16[512,64]{0,1:T(8,128)(2,1)S(1)}, bf16[512,64]{0,1:T(8,128)(2,1)}, u32[]{:S(2)}) copy-start(bf16[512,64]{0,1:T(8,128)(2,1)} %copy-done.36) | copy-start | bytes 196612
  345.7 124.3 %all-reduce.17.cloned.1.call-start = ((), (), s32[]{:S(2)}) async-start(), calls=%async_computation.21 | async-start | bytes 4194304 | tf_op jit(solution)/shard_map/psum | solution.py:149
  349.3 159.3 %reduce-scatter.16.cloned.1.call-start = ((), (), s32[]{:S(2)}) async-start(), calls=%async_computation.16 | async-start | bytes 1179648 | tf_op jit(solution)/shard_map/reduce_scatter | solution.py:282
  353.3 210.6 %reduce-scatter.20.cloned.1.call-start = ((), (), s32[]{:S(2)}) async-start(), calls=%async_computation.18 | async-start | bytes 4718592 | tf_op jit(solution)/shard_map/reduce_scatter | solution.py:288
  359.0 260.4 %reduce-scatter.18.cloned.1.call-start = ((), (), s32[]{:S(2)}) async-start(), calls=%async_computation.17 | async-start | bytes 4718592 | tf_op jit(solution)/shard_map/reduce_scatter | solution.py:286
  364.0 305.4 %reduce-scatter.14.cloned.1.call-start = ((), (), s32[]{:S(2)}) async-start(), calls=%async_computation.15 | async-start | bytes 3538944 | tf_op jit(solution)/shard_map/reduce_scatter | solution.py:280
  368.6 103.6 %copy-start.49 = (f32[1024]{0:T(1024)S(1)}, f32[1024]{0:T(1024)}, u32[]{:S(2)}) copy-start(f32[1024]{0:T(1024)} %get-tuple-element.14) | copy-start | bytes 12292
  368.6 103.6 %copy-start.50 = (f32[1024]{0:T(1024)S(1)}, f32[1024]{0:T(1024)}, u32[]{:S(2)}) copy-start(f32[1024]{0:T(1024)} %get-tuple-element.22) | copy-start | bytes 12292
  368.6 103.6 %copy-start.51 = (f32[1024]{0:T(1024)S(1)}, f32[1024]{0:T(1024)}, u32[]{:S(2)}) copy-start(f32[1024]{0:T(1024)} %get-tuple-element.44) | copy-start | bytes 12292
  368.6 103.6 %copy-start.52 = (f32[1024]{0:T(1024)S(1)}, f32[1024]{0:T(1024)}, u32[]{:S(2)}) copy-start(f32[1024]{0:T(1024)} %get-tuple-element.50) | copy-start | bytes 12292
  368.6 103.6 %copy-start.54 = (f32[1024]{0:T(1024)S(1)}, f32[1024]{0:T(1024)}, u32[]{:S(2)}) copy-start(f32[1024]{0:T(1024)} %get-tuple-element.63) | copy-start | bytes 12292
  (50 other events, 209.3 us)
Sparse Core Ops, SparseCore 0:
  10.5 28.5 all-gather.14
  43.8 17.5 all-gather.22
  64.6 16.7 all-gather.16
  93.2 51.8 all-reduce.12
  147.0 27.2 all-gather.18
  176.2 28.1 all-gather.20
  214.0 51.7 all-reduce.14
  281.6 24.2 reduce-scatter.11
  319.2 24.2 reduce-scatter.9
  346.3 33.4 reduce-scatter.21
  382.9 87.0 all-reduce.16
  473.6 34.9 reduce-scatter.15
  512.5 51.2 reduce-scatter.19
  568.0 51.3 reduce-scatter.17
  623.2 46.2 reduce-scatter.13
where the time goes:
time: 684 us; the launch traced here: 676 us
  waiting for transfers between devices  406 us (59%)
  blocking collectives  103 us (15%)
  matrix products  86.7 us (13%)
  other arithmetic  38.3 us (6%)
  local copies, waits for them, and re-layouts  24.6 us (4%)
  between operations  15.6 us (2%)
    psum x1, waiting for transfers between devices, body(): mlp_out = lax.psum(mlp_part.astype(jnp.bfloat16), 'tp').astype(jnp.float32)  88.9 us
    reduce_scatter x1, waiting for transfers between devices, body(): lax.psum_scatter(grad_expand_w, ('dp', 'ctx'), scatter_dimension=0, tiled...  55.5 us
    reduce_scatter x1, waiting for transfers between devices, body(): lax.psum_scatter(grad_shrink_w, ('dp', 'ctx'), scatter_dimension=1, tiled...  55.3 us
    psum x1, waiting for transfers between devices, body(): lax.psum(normed2_part.astype(jnp.bfloat16), 'tp').astype(jnp.float32)  51.6 us
    reduce_scatter x1, waiting for transfers between devices, body(): lax.psum_scatter(grad_attend_w, ('dp', 'ctx'), scatter_dimension=0, tiled...  50.1 us
    all_gather x1, waiting for transfers between devices, body(): lax.all_gather(expand_weight, ('dp', 'ctx'), axis=0, tiled=True)  26.9 us
    all_gather x1, waiting for transfers between devices, body(): lax.all_gather(shrink_weight, ('dp', 'ctx'), axis=1, tiled=True)  25.9 us
    unnamed x1, blocking collectives  24.2 us
  transfers between devices with their start and end apart: 15, of which 13 were waited for; matrix products, arithmetic and copies ran while one was open for 14% of the time, Pallas kernels for 0%

commit v1 on v0

--- a/solution.py
+++ b/solution.py
@@ -146,7 +146,9 @@
     mlp_part = jnp.einsum(
         "sqf,fd->sqd", activation, shrink_full, preferred_element_type=jnp.float32
     )
-    mlp_out = lax.psum(mlp_part.astype(jnp.bfloat16), "tp").astype(jnp.float32)
+    mlp_out = jnp.sum(lax.all_gather(mlp_part.astype(jnp.bfloat16), "tp"), axis=0).astype(
+        jnp.float32
+    )
     layer_output = (hidden + mlp_out + shrink_add).astype(jnp.bfloat16)
     back_params = (
         lax.all_gather(norm1_gain, ("dp", "ctx"), axis=0, tiled=True),

time: 684 us -> 734 us (1.073)
  waiting for transfers between devices: 406 us -> 447 us
    all_gather x0 -> x1, waiting for transfers between devices: none -> 79.3 us  [body(): lax.all_gather(mlp_part.astype(jnp.bfloat16), 'tp')]
    psum x1, waiting for transfers between devices: 88.9 us -> 53.4 us  [body(): lax.psum(normed1_part.astype(jnp.bfloat16), 'tp').astype(jnp.float32)]
    reduce_scatter x1, waiting for transfers between devices: 4.46 us -> 39.6 us  [body(): lax.psum_scatter(grad_merge_w, ('dp', 'ctx'), scatter_dimension=1, tiled=...]
    reduce_scatter x1, waiting for transfers between devices: 55.5 us -> 21.1 us  [body(): lax.psum_scatter(grad_expand_w, ('dp', 'ctx'), scatter_dimension=0, tiled...]
    psum x1, waiting for transfers between devices: 51.6 us -> 38 us  [body(): lax.psum(normed2_part.astype(jnp.bfloat16), 'tp').astype(jnp.float32)]
    unnamed x16 -> x17, waiting for transfers between devices: 1.85 us -> 10.5 us
    unnamed x145 -> x151, local copies, waits for them, and re-layouts: 23.8 us -> 24.5 us
  transfers between devices with their start and end apart: 15 -> 16, of which waited for: 13 -> 14; matrix products, arithmetic and copies ran while one was open for 14% -> 14% of each run, Pallas kernels for 0% -> 0%
where the time goes in v1:
time: 734 us; the launch traced here: 726 us
  waiting for transfers between devices  447 us (61%)
  blocking collectives  104 us (14%)
  matrix products  89.4 us (12%)
  other arithmetic  44.5 us (6%)
  local copies, waits for them, and re-layouts  25.3 us (3%)
  between operations  15.7 us (2%)
    all_gather x1, waiting for transfers between devices, body(): lax.all_gather(mlp_part.astype(jnp.bfloat16), 'tp')  79.3 us
    reduce_scatter x1, waiting for transfers between devices, body(): lax.psum_scatter(grad_shrink_w, ('dp', 'ctx'), scatter_dimension=1, tiled...  55.5 us
    psum x1, waiting for transfers between devices, body(): lax.psum(normed1_part.astype(jnp.bfloat16), 'tp').astype(jnp.float32)  53.4 us
    reduce_scatter x1, waiting for transfers between devices, body(): lax.psum_scatter(grad_attend_w, ('dp', 'ctx'), scatter_dimension=0, tiled...  50.1 us
    reduce_scatter x1, waiting for transfers between devices, body(): lax.psum_scatter(grad_merge_w, ('dp', 'ctx'), scatter_dimension=1, tiled=...  39.6 us
    psum x1, waiting for transfers between devices, body(): lax.psum(normed2_part.astype(jnp.bfloat16), 'tp').astype(jnp.float32)  38 us
    all_gather x1, waiting for transfers between devices, body(): lax.all_gather(expand_weight, ('dp', 'ctx'), axis=0, tiled=True)  26.9 us
    all_gather x1, waiting for transfers between devices, body(): lax.all_gather(shrink_weight, ('dp', 'ctx'), axis=1, tiled=True)  25.8 us
  transfers between devices with their start and end apart: 16, of which 14 were waited for; matrix products, arithmetic and copies ran while one was open for 14% of the time, Pallas kernels for 0%

profile of v1, /device:TPU:0, one launch (start us, length us, event | category | flops | bytes accessed | tf_op | source)
XLA Modules:
  0.0 726.4 jit_solution(8351556863834214100)
XLA Ops:
  9.1 10.3 %all-gather.2 = bf16[8,1,128]{2,1,0:T(2,128)(2,1)S(1)} all-gather(bf16[1,1,128]{2,1,0:T(2,128)(2,1)} %bitcast.296), channel_id=1, replica_groups=mesh['dp'=2,'ctx'=4,'tp'=4] {'dp','ctx'}, dimensions={0}, use_global_device_ids=true | all-gather | bytes 2304 | tf_op jit(solution)/shard_map/all_gather | solution.py:57
  19.4 8.6 %all-gather.3 = bf16[8,1,128]{2,1,0:T(2,128)(2,1)S(1)} all-gather(bf16[1,1,128]{2,1,0:T(2,128)(2,1)} %bitcast.297), channel_id=1, replica_groups=mesh['dp'=2,'ctx'=4,'tp'=4] {'dp','ctx'}, dimensions={0}, use_global_device_ids=true | all-gather | bytes 2304 | tf_op jit(solution)/shard_map/all_gather | solution.py:58
  29.9 9.1 %all-gather.17.cloned.1.call-done = bf16[1024,3,256]{0,2,1:T(8,128)(2,1)} async-done(((bf16[128,3,256]{0,2,1:T(8,128)(2,1)}), bf16[1024,3,256]{0,2,1:T(8,128)(2,1)}) %all-gather.17.cloned.1.call-update) | async-done | bytes 1572880 | tf_op jit(solution)/shard_map/all_gather | solution.py:59
  43.7 8.7 %all-gather.4 = bf16[8,32,2]{1,2,0:T(2,128)(2,1)S(1)} all-gather(bf16[1,32,2]{1,2,0:T(2,128)(2,1)S(1)} %bitcast.298), channel_id=1, replica_groups=mesh['dp'=2,'ctx'=4,'tp'=4] {'dp','ctx'}, dimensions={0}, use_global_device_ids=true | all-gather | bytes 1152 | tf_op jit(solution)/shard_map/all_gather | solution.py:60
  52.6 9.8 %all_gather.62 = bf16[256,1024]{1,0:T(8,128)(2,1)S(1)} all-gather(bf16[256,128]{1,0:T(8,128)(2,1)S(1)} %copy-done.41), channel_id=1, replica_groups=mesh['dp'=2,'ctx'=4,'tp'=4] {'dp','ctx'}, dimensions={1}, use_global_device_ids=true | all-gather | bytes 589824 | tf_op jit(solution)/shard_map/all_gather | solution.py:61
  73.6 4.4 fusion.2
  94.3 8.7 %all-gather.5 = bf16[8,1,128]{2,1,0:T(2,128)(2,1)S(1)} all-gather(bf16[1,1,128]{2,1,0:T(2,128)(2,1)S(1)} %bitcast.299), channel_id=1, replica_groups=mesh['dp'=2,'ctx'=4,'tp'=4] {'dp','ctx'}, dimensions={0}, use_global_device_ids=true | all-gather | bytes 2304 | tf_op jit(solution)/shard_map/all_gather | solution.py:62
  103.1 7.8 %all-gather.6 = bf16[8,1,128]{2,1,0:T(2,128)(2,1)S(1)} all-gather(bf16[1,1,128]{2,1,0:T(2,128)(2,1)S(1)} %bitcast.300), channel_id=1, replica_groups=mesh['dp'=2,'ctx'=4,'tp'=4] {'dp','ctx'}, dimensions={0}, use_global_device_ids=true | all-gather | bytes 2304 | tf_op jit(solution)/shard_map/all_gather | solution.py:63
  110.8 8.7 %all-gather.7 = bf16[8,1,128]{2,1,0:T(2,128)(2,1)S(1)} all-gather(bf16[1,1,128]{2,1,0:T(2,128)(2,1)S(1)} %bitcast.301), channel_id=1, replica_groups=mesh['dp'=2,'ctx'=4,'tp'=4] {'dp','ctx'}, dimensions={0}, use_global_device_ids=true | all-gather | bytes 2304 | tf_op jit(solution)/shard_map/all_gather | solution.py:64
  119.5 8.0 %all-gather.8 = bf16[8,1,128]{2,1,0:T(2,128)(2,1)S(1)} all-gather(bf16[1,1,128]{2,1,0:T(2,128)(2,1)S(1)} %bitcast.302), channel_id=1, replica_groups=mesh['dp'=2,'ctx'=4,'tp'=4] {'dp','ctx'}, dimensions={0}, use_global_device_ids=true | all-gather | bytes 2304 | tf_op jit(solution)/shard_map/all_gather | solution.py:66
  127.6 17.5 %all-reduce.12.cloned.1.call-done = bf16[1,512,1024]{2,1,0:T(8,128)(2,1)} async-done(((bf16[1,512,1024]{2,1,0:T(8,128)(2,1)}), bf16[1,512,1024]{2,1,0:T(8,128)(2,1)}) %all-reduce.12.cloned.1.call-update) | async-done | bytes 1048592 | tf_op jit(solution)/shard_map/psum | solution.py:136
  147.4 26.9 %all-gather.21.cloned.1.call-done = bf16[1024,1024]{1,0:T(8,128)(2,1)} async-done(((bf16[128,1024]{1,0:T(8,128)(2,1)}), bf16[1024,1024]{1,0:T(8,128)(2,1)}) %all-gather.21.cloned.1.call-update) | async-done | bytes 2097168 | tf_op jit(solution)/shard_map/all_gather | solution.py:65
  178.6 25.8 %all-gather.23.cloned.1.call-done = bf16[1024,1024]{1,0:T(8,128)(2,1)} async-done(((bf16[1024,128]{1,0:T(8,128)(2,1)}), bf16[1024,1024]{1,0:T(8,128)(2,1)}) %all-gather.23.cloned.1.call-update) | async-done | bytes 2097168 | tf_op jit(solution)/shard_map/all_gather | solution.py:67
  204.4 6.1 convert_reduce_fusion.3
  213.9 4.7 convolution_convert_fusion.5
  218.7 9.1 %all-gather.9 = bf16[8,1,128]{2,1,0:T(2,128)(2,1)S(1)} all-gather(bf16[1,1,128]{2,1,0:T(2,128)(2,1)S(1)} %bitcast.303), channel_id=1, replica_groups=mesh['dp'=2,'ctx'=4,'tp'=4] {'dp','ctx'}, dimensions={0}, use_global_device_ids=true | all-gather | bytes 2304 | tf_op jit(solution)/shard_map/all_gather | solution.py:68
  227.8 38.0 %all-reduce.14.cloned.1.call-done = bf16[1,512,1024]{2,1,0:T(8,128)(2,1)} async-done(((bf16[1,512,1024]{2,1,0:T(8,128)(2,1)}), bf16[1,512,1024]{2,1,0:T(8,128)(2,1)}) %all-reduce.14.cloned.1.call-update) | async-done | bytes 1048592 | tf_op jit(solution)/shard_map/psum | solution.py:193
  268.8 79.3 %all-gather.27.cloned.1.call-done = bf16[2048,1024]{1,0:T(8,128)(2,1)} async-done(((bf16[512,1024]{1,0:T(8,128)(2,1)}), bf16[2048,1024]{1,0:T(8,128)(2,1)}) %all-gather.27.cloned.1.call-update) | async-done | bytes 4194320 | tf_op jit(solution)/shard_map/all_gather | solution.py:149
  348.1 4.4 reduce.40
  352.5 4.6 fusion.132
  377.2 9.0 %multiply_reduce_fusion.3 = (f32[512]{0:T(512)S(1)}, f32[512]{0:T(512)S(1)}, f32[512]{0:T(512)S(1)}, f32[512]{0:T(512)S(1)}, f32[512,2048]{1,0:T(8,128)}) fusion(f32[512]{0:T(512)S(1)} %get-tuple-element.65, f32[512,2048]{1,0:T(8,128)} %copy-done.21, s32[512]{0:T(512)S(1)} %iota_add_fusion, s32[2048]{0:T(1024)S(1)} %bitcast.256, s32[512]{0:T(512)S(1)} %bitcast.277, ...), kind=kOutput, calls=%fused_computation.10 | convolution fusion | flops 158332928 | bytes 33910784 | tf_op jit(solution)/shard_map/sqd,skd->sqk/dot_general | solution.py:228
  386.2 13.2 %multiply_convert_fusion.3 = (bf16[512,2048]{1,0:T(8,128)(2,1)}, bf16[512,2048]{1,0:T(8,128)(2,1)}, bf16[512,2048]{1,0:T(8,128)(2,1)}, bf16[512,2048]{1,0:T(8,128)(2,1)}) fusion(f32[512,2048]{1,0:T(8,128)} %get-tuple-element.59, f32[512]{0:T(512)S(1)} %get-tuple-element.24, f32[512]{0:T(512)S(1)} %get-tuple-element.65, f32[512,2048]{1,0:T(8,128)} %copy-done.21, ...), kind=kLoop, calls=%fused_computation.9 | loop fusion | flops 28311552 | bytes 41971712 | tf_op jit(solution)/shard_map/convert_element_type | solution.py:232
  412.2 16.4 %reduce-scatter.10.cloned.1.call-done = bf16[1,512,256]{1,2,0:T(8,128)(2,1)} async-done(((bf16[1,2048,256]{1,2,0:T(8,128)(2,1)}), bf16[1,512,256]{1,2,0:T(8,128)(2,1)}) %reduce-scatter.10.cloned.1.call-update) | async-done | bytes 262160 | tf_op jit(solution)/shard_map/reduce_scatter | solution.py:247
  434.7 4.6 fusion.120
  440.6 5.3 fusion.91
  455.8 9.2 %reduce-scatter.22.cloned.1.call-done = f32[32,2]{1,0:T(8,128)} async-done(((f32[256,2]{1,0:T(8,128)}), f32[32,2]{1,0:T(8,128)}) %reduce-scatter.22.cloned.1.call-update) | async-done | bytes 272
  466.3 53.4 %all-reduce.16.cloned.1.call-done = bf16[1,512,1024]{2,1,0:T(8,128)(2,1)} async-done(((bf16[1,512,1024]{2,1,0:T(8,128)(2,1)}), bf16[1,512,1024]{2,1,0:T(8,128)(2,1)}) %all-reduce.16.cloned.1.call-update) | async-done | bytes 1048592 | tf_op jit(solution)/shard_map/psum | solution.py:273
  522.0 24.2 %all-reduce.7 = (f32[1024]{0:T(1024)S(1)}, f32[1024]{0:T(1024)S(1)}, f32[1024]{0:T(1024)S(1)}, f32[1024]{0:T(1024)S(1)}, f32[1024]{0:T(1024)S(1)}, /*index=5*/f32[1024]{0:T(1024)S(1)}, f32[1024]{0:T(1024)S(1)}) all-reduce(f32[1024]{0:T(1024)S(1)} %get-tuple-element.16, ...), channel_id=6, replica_groups=mesh['dp'=2,'ctx'=4,'tp'=4] {'dp','ctx'}, use_global_device_ids=true, to_apply=%region_27.28.clone | all-reduce | flops 7168 | bytes 57344
  553.3 21.1 %reduce-scatter.18.cloned.1.call-done = f32[128,1024]{1,0:T(8,128)} async-done(((f32[1024,1024]{1,0:T(8,128)}), f32[128,1024]{1,0:T(8,128)}) %reduce-scatter.18.cloned.1.call-update) | async-done | bytes 524304 | tf_op jit(solution)/shard_map/reduce_scatter | solution.py:288
  574.4 55.5 %reduce-scatter.20.cloned.1.call-done = f32[1024,128]{1,0:T(8,128)} async-done(((f32[1024,1024]{1,0:T(8,128)}), f32[1024,128]{1,0:T(8,128)}) %reduce-scatter.20.cloned.1.call-update) | async-done | bytes 524304 | tf_op jit(solution)/shard_map/reduce_scatter | solution.py:290
  629.9 39.6 %reduce-scatter.16.cloned.1.call-done = f32[256,128]{1,0:T(8,128)} async-done(((f32[256,1024]{1,0:T(8,128)}), f32[256,128]{1,0:T(8,128)}) %reduce-scatter.16.cloned.1.call-update) | async-done | bytes 131088 | tf_op jit(solution)/shard_map/reduce_scatter | solution.py:284
  669.6 50.1 %reduce-scatter.14.cloned.1.call-done = f32[128,3,256]{2,0,1:T(8,128)} async-done(((f32[1024,3,256]{2,0,1:T(8,128)}), f32[128,3,256]{2,0,1:T(8,128)}) %reduce-scatter.14.cloned.1.call-update) | async-done | bytes 393232 | tf_op jit(solution)/shard_map/reduce_scatter | solution.py:282
  (253 shorter events, 108.4 us)
Async XLA Ops:
  7.2 22.3 %copy-start = (bf16[1,512,1024]{2,1,0:T(8,128)(2,1)S(1)}, bf16[1,512,1024]{2,1,0:T(8,128)(2,1)}, u32[]{:S(2)}) copy-start(bf16[1,512,1024]{2,1,0:T(8,128)(2,1)} %param.15) | copy-start | bytes 3145732
  7.2 31.9 %all-gather.17.cloned.1.call-start = ((), (), s32[]{:S(2)}) async-start(), calls=%async_computation.7 | async-start | bytes 1769472 | tf_op jit(solution)/shard_map/all_gather | solution.py:59
  9.1 55.4 %all-gather.25.cloned.1.call-start = ((), (), s32[]{:S(2)}) async-start(), calls=%async_computation.20 | async-start | bytes 1310720 | tf_op jit(solution)/shard_map/all_gather | solution.py:98
  43.7 37.7 %all-gather.19.cloned.1.call-start = ((), (), s32[]{:S(2)}) async-start(), calls=%async_computation.8 | async-start | bytes 1310720 | tf_op jit(solution)/shard_map/all_gather | solution.py:99
  52.6 300.0 %copy-start.52 = (f32[1,512]{1,0:T(1,128)}, f32[1,512]{1,0:T(1,128)S(1)}, u32[]{:S(2)}) copy-start(f32[1,512]{1,0:T(1,128)S(1)} %get-tuple-element.44) | copy-start | bytes 6148
  64.5 80.6 %all-reduce.12.cloned.1.call-start = ((), (), s32[]{:S(2)}) async-start(), calls=%async_computation.9 | async-start | bytes 2097152 | tf_op jit(solution)/shard_map/psum | solution.py:136
  91.6 55.2 %copy-start.39 = (bf16[512,64]{0,1:T(8,128)(2,1)}, bf16[512,64]{0,1:T(8,128)(2,1)S(1)}, u32[]{:S(2)}) copy-start(bf16[512,64]{0,1:T(8,128)(2,1)S(1)} %fusion.74) | copy-start | bytes 196612
  91.6 19.2 %copy-start.64 = (bf16[128]{0:T(256)(128)(2,1)S(1)}, bf16[128]{0:T(256)(128)(2,1)}, u32[]{:S(2)}) copy-start(bf16[128]{0:T(256)(128)(2,1)} %param.25) | copy-start | bytes 772
  91.6 27.9 %copy-start.65 = (bf16[128]{0:T(256)(128)(2,1)S(1)}, bf16[128]{0:T(256)(128)(2,1)}, u32[]{:S(2)}) copy-start(bf16[128]{0:T(256)(128)(2,1)} %param.27) | copy-start | bytes 772
  93.1 81.2 %all-gather.21.cloned.1.call-start = ((), (), s32[]{:S(2)}) async-start(), calls=%async_computation.10 | async-start | bytes 2359296 | tf_op jit(solution)/shard_map/all_gather | solution.py:65
  93.7 110.7 %all-gather.23.cloned.1.call-start = ((), (), s32[]{:S(2)}) async-start(), calls=%async_computation.11 | async-start | bytes 2359296 | tf_op jit(solution)/shard_map/all_gather | solution.py:67
  94.3 171.5 %all-reduce.14.cloned.1.call-start = ((), (), s32[]{:S(2)}) async-start(), calls=%async_computation.12 | async-start | bytes 2097152 | tf_op jit(solution)/shard_map/psum | solution.py:193
  119.5 54.8 %copy-start.59 = (f32[8,1,128]{2,1,0:T(1,128)}, f32[8,1,128]{2,1,0:T(1,128)S(1)}, u32[]{:S(2)}) copy-start(f32[8,1,128]{2,1,0:T(1,128)S(1)} %convert_element_type.314) | copy-start | bytes 12292
  127.5 86.4 %copy-start.57 = (f32[8,1,128]{2,1,0:T(1,128)}, f32[8,1,128]{2,1,0:T(1,128)S(1)}, u32[]{:S(2)}) copy-start(f32[8,1,128]{2,1,0:T(1,128)S(1)} %convert_element_type.315) | copy-start | bytes 12292
  146.8 205.7 %copy-start.42 = (f32[512]{0:T(512)}, f32[512]{0:T(512)S(1)}, u32[]{:S(2)}) copy-start(f32[512]{0:T(512)S(1)} %broadcast_multiply_fusion.4) | copy-start | bytes 6148
  147.4 205.1 %copy-start.44 = (f32[512]{0:T(512)}, f32[512]{0:T(512)S(1)}, u32[]{:S(2)}) copy-start(f32[512]{0:T(512)S(1)} %add_rsqrt_fusion) | copy-start | bytes 6148
  213.9 134.3 %all-gather.27.cloned.1.call-start = ((), (), s32[]{:S(2)}) async-start(), calls=%async_computation.21 | async-start | bytes 5242880 | tf_op jit(solution)/shard_map/all_gather | solution.py:149
  218.6 193.6 %reduce-scatter.12.cloned.1.call-start = ((), (), s32[]{:S(2)}) async-start(), calls=%async_computation.14 | async-start | bytes 1310720 | tf_op jit(solution)/shard_map/reduce_scatter | solution.py:253
  367.5 61.1 %reduce-scatter.10.cloned.1.call-start = ((), (), s32[]{:S(2)}) async-start(), calls=%async_computation.13 | async-start | bytes 1310720 | tf_op jit(solution)/shard_map/reduce_scatter | solution.py:247
  405.0 60.0 %reduce-scatter.22.cloned.1.call-start = ((), (), s32[]{:S(2)}) async-start(), calls=%async_computation.22 | async-start | bytes 147456
  412.2 18.6 %copy-start.33 = (bf16[512,64]{0,1:T(8,128)(2,1)S(1)}, bf16[512,64]{0,1:T(8,128)(2,1)}, u32[]{:S(2)}) copy-start(bf16[512,64]{0,1:T(8,128)(2,1)} %copy-done.32) | copy-start | bytes 196612
  412.2 18.6 %copy-start.35 = (bf16[512,64]{0,1:T(8,128)(2,1)S(1)}, bf16[512,64]{0,1:T(8,128)(2,1)}, u32[]{:S(2)}) copy-start(bf16[512,64]{0,1:T(8,128)(2,1)} %copy-done.34) | copy-start | bytes 196612
  430.8 89.0 %all-reduce.16.cloned.1.call-start = ((), (), s32[]{:S(2)}) async-start(), calls=%async_computation.15 | async-start | bytes 2097152 | tf_op jit(solution)/shard_map/psum | solution.py:273
  434.4 140.0 %reduce-scatter.18.cloned.1.call-start = ((), (), s32[]{:S(2)}) async-start(), calls=%async_computation.18 | async-start | bytes 4718592 | tf_op jit(solution)/shard_map/reduce_scatter | solution.py:288
  439.3 190.6 %reduce-scatter.20.cloned.1.call-start = ((), (), s32[]{:S(2)}) async-start(), calls=%async_computation.19 | async-start | bytes 4718592 | tf_op jit(solution)/shard_map/reduce_scatter | solution.py:290
  445.9 223.6 %reduce-scatter.16.cloned.1.call-start = ((), (), s32[]{:S(2)}) async-start(), calls=%async_computation.17 | async-start | bytes 1179648 | tf_op jit(solution)/shard_map/reduce_scatter | solution.py:284
  449.9 269.8 %reduce-scatter.14.cloned.1.call-start = ((), (), s32[]{:S(2)}) async-start(), calls=%async_computation.16 | async-start | bytes 3538944 | tf_op jit(solution)/shard_map/reduce_scatter | solution.py:282
  453.9 68.1 %copy-start.48 = (f32[1024]{0:T(1024)S(1)}, f32[1024]{0:T(1024)}, u32[]{:S(2)}) copy-start(f32[1024]{0:T(1024)} %get-tuple-element.42) | copy-start | bytes 12292
  453.9 68.1 %copy-start.49 = (f32[1024]{0:T(1024)S(1)}, f32[1024]{0:T(1024)}, u32[]{:S(2)}) copy-start(f32[1024]{0:T(1024)} %get-tuple-element.49) | copy-start | bytes 12292
  453.9 68.1 %copy-start.50 = (f32[1024]{0:T(1024)S(1)}, f32[1024]{0:T(1024)}, u32[]{:S(2)}) copy-start(f32[1024]{0:T(1024)} %get-tuple-element.14) | copy-start | bytes 12292
  453.9 68.1 %copy-start.51 = (f32[1024]{0:T(1024)S(1)}, f32[1024]{0:T(1024)}, u32[]{:S(2)}) copy-start(f32[1024]{0:T(1024)} %get-tuple-element.22) | copy-start | bytes 12292
  453.9 68.1 %copy-start.54 = (f32[1024]{0:T(1024)S(1)}, f32[1024]{0:T(1024)}, u32[]{:S(2)}) copy-start(f32[1024]{0:T(1024)} %get-tuple-element.60) | copy-start | bytes 12292
  (54 other events, 239.2 us)
Sparse Core Ops, SparseCore 0:
  10.5 28.5 all-gather.16
  43.8 17.5 all-gather.24
  64.6 16.7 all-gather.18
  93.2 51.8 all-reduce.11
  147.0 27.2 all-gather.20
  176.2 28.1 all-gather.22
  214.0 51.7 all-reduce.13
  268.0 80.1 all-gather.26
  367.6 23.3 reduce-scatter.11
  405.1 23.4 reduce-scatter.9
  431.6 33.3 reduce-scatter.21
  467.9 51.8 all-reduce.15
  523.6 50.6 reduce-scatter.17
  578.5 51.3 reduce-scatter.19
  633.5 35.9 reduce-scatter.15
  673.4 46.2 reduce-scatter.13
